TPU v7x, 512 devices: a whole 4x8x8 slice. The times are simulated.
512 devices in a mesh: grp: 16 (over y_hi, x), pen: 32 (over y_lo, z, core).
Axes of the slice: x: 4, y: 8 (y_hi: 4, y_lo: 2; y = y_hi * 2 + y_lo), z: 8, core: 2. Of those that a mesh axis runs over, the one named last changes fastest.
Arguments:
- flow_fields: float32 [4, 16, 1536, 1536], P(None, 'grp', 'pen'), may hold values from -6 to 6
- marker_cells: int32 [16, 32, 1024, 8], P('grp', 'pen'), may hold values from 0 to 73727
- marker_weights: float32 [16, 32, 1024, 8], P('grp', 'pen'), may hold values from 0.05 to 0.3
- solid_blocks: int32 [16, 1536, 12], P('grp', 'pen'), may hold values 0 or 1
Outputs:
- velocity_next: float32 [3, 16, 1536, 1536], P(None, 'grp', 'pen')
- poisson_source: float32 [16, 1536, 1536], P(None, 'pen', 'grp')
Inputs may be any that keep to these rules, and one draw needn't show every extreme that they name: `marker_cells`: each entry numbers a cell of the device's own home block of 73728 cells, first dimension slowest, third fastest.
All inputs are finite; a program needn't handle non-finite values. No bound on the sum of `solid_blocks` on one device may be relied on, other than what follows from the above.
Results may differ from a plain program's by a relative error of at most 0.0003.
Values sent between devices are 32-bit elements; how exact they have to be, the bound alone decides.
A program may use at most 128 MiB of HBM per device.

v0:
```python
import math

import jax
import jax.numpy as jnp
from jax import lax
from jax.sharding import PartitionSpec as P


def compact(line_data):
    length = line_data.shape[0]
    padded = jnp.pad(line_data, ((2, 2), (0, 0)))
    source = 14.0 / 9.0 * 0.5 * (padded[3:-1] - padded[1:-3]) + 1.0 / 9.0 * 0.25 * (
        padded[4:] - padded[:-4]
    )
    lower_band = jnp.full((length,), 1.0 / 3.0, dtype=line_data.dtype).at[0].set(0.0)
    upper_band = jnp.full((length,), 1.0 / 3.0, dtype=line_data.dtype).at[length - 1].set(0.0)
    middle_band = jnp.ones((length,), dtype=line_data.dtype)
    return lax.linalg.tridiagonal_solve(lower_band, middle_band, upper_band, source)


def compact_along(block_data, axis):
    reordered = jnp.moveaxis(block_data, axis, 0)
    shaped = reordered.shape
    result = compact(reordered.reshape(shaped[0], -1)).reshape(shaped)
    return jnp.moveaxis(result, 0, axis)


def circulant_block(lag_block, block_width, length):
    out_rows = lax.iota(jnp.int32, block_width)
    in_columns = lax.iota(jnp.int32, block_width)
    offset = (lag_block * block_width + out_rows[:, None] - in_columns[None, :]) % length
    phases = math.pi / length * offset.astype(jnp.float32)
    parity = (1 - 2 * (offset % 2)).astype(jnp.float32)
    nonzero = offset != 0
    sine_values = jnp.where(nonzero, jnp.sin(phases), 1.0)
    return jnp.where(nonzero, math.pi / length * parity * jnp.cos(phases) / sine_values, 0.0)


def spectral_along(block_data, axis):
    reordered = jnp.moveaxis(block_data, axis, -1)
    shaped = reordered.shape
    length = shaped[-1]
    block_width = math.gcd(length, 384)
    block_count = length // block_width
    line_blocks = reordered.reshape(-1, block_count, block_width)
    result = jnp.zeros_like(line_blocks)
    for lag_block in range(block_count):
        table_block = circulant_block(lag_block, block_width, length)
        shifted = jnp.roll(line_blocks, lag_block, axis=1)
        result = result + jnp.einsum(
            "xas,rs->xar",
            shifted,
            table_block,
            precision=lax.Precision.HIGHEST,
            preferred_element_type=jnp.float32,
        )
    return jnp.moveaxis(result.reshape(shaped), -1, axis)


def terms_for(fields, slopes, direction):
    carried = -fields[direction][None] * slopes[:3]
    return carried.at[direction].add(-slopes[3])


def body(flow_fields, marker_cells, marker_weights, solid_blocks):
    slopes_z = spectral_along(flow_fields, 3)
    tendency = terms_for(flow_fields, slopes_z, 2)
    pencil = lax.all_to_all(flow_fields, "pen", split_axis=3, concat_axis=2, tiled=True)
    slopes = spectral_along(pencil, 2)
    returned = jnp.concatenate([terms_for(pencil, slopes, 1), slopes[1][None]], axis=0)
    second_part = lax.all_to_all(returned, "pen", split_axis=2, concat_axis=3, tiled=True)
    tendency = tendency + second_part[:3]
    pencil = lax.all_to_all(flow_fields, "grp", split_axis=3, concat_axis=1, tiled=True)
    slopes = compact_along(pencil, 1)
    returned = jnp.concatenate([terms_for(pencil, slopes, 0), slopes[0][None]], axis=0)
    first_part = lax.all_to_all(returned, "grp", split_axis=1, concat_axis=3, tiled=True)
    tendency = tendency + first_part[:3]
    divergence = slopes_z[2] + second_part[3] + first_part[3]
    poisson_source = lax.all_to_all(divergence, "grp", split_axis=2, concat_axis=0, tiled=True)
    provisional = flow_fields[:3] + 0.1 * tendency
    shaped = provisional.shape
    flattened = provisional.reshape(3, -1)
    cells_index = marker_cells[0, 0].reshape(-1)
    weights = marker_weights[0, 0]
    gathered = flattened[:, cells_index].reshape(3, weights.shape[0], weights.shape[1])
    sampled = jnp.sum(gathered * weights[None], axis=2)
    spread = (sampled[..., None] * weights[None]).reshape(3, -1)
    correction = jnp.zeros_like(flattened).at[:, cells_index].add(spread).reshape(shaped)
    block_cells = flow_fields.shape[3] // solid_blocks.shape[2]
    solid = jnp.repeat(solid_blocks, block_cells, axis=2).astype(jnp.float32)
    velocity_next = (1.0 - solid)[None] * (provisional - correction)
    return (velocity_next, poisson_source)


def solution(mesh):
    return jax.shard_map(
        body,
        mesh=mesh,
        in_specs=(
            P(None, "grp", "pen", None),
            P("grp", "pen", None, None),
            P("grp", "pen", None, None),
            P("grp", "pen", None),
        ),
        out_specs=(P(None, "grp", "pen", None), P(None, "pen", "grp")),
        check_vma=False,
    )
```

profile of v0, /device:TPU:1, one launch (start us, length us, event | category | flops | bytes accessed | tf_op | source)
XLA Modules:
  0.0 412.1 jit_solution(2675801242251828459)
XLA Ops:
  7.9 10.8 %all-to-all-start.2 = ((f32[16,1,18432]{2,1,0:T(1,128)}), f32[16,1,18432]{2,1,0:T(1,128)}, u32[]{:S(2)}, u32[]{:S(2)}) async-start(f32[16,1,18432]{2,1,0:T(1,128)} %reshape.477), calls=%async_computation.2 | async-start | bytes 2359296 | tf_op jit(solution)/shard_map/all_to_all | solution.py:73
  24.3 6.0 %convolution_bitcast_fusion.1 = f32[192,4,384]{2,0,1:T(8,128)} fusion(f32[192,4,384]{2,1,0:T(4,128)S(1)} %copy-done), kind=kOutput, calls=%fused_computation.24 | convolution fusion | flops 1363230720 | bytes 2359296 | tf_op jit(solution)/shard_map/xas,rs->xar/dot_general | solution.py:50
  47.8 4.5 %reshape.479 = f32[32,1,9216]{2,1,0:T(1,128)} reshape(f32[1536,1,4,48]{3,2,1,0:T(4,128)S(1)} %bitcast.123) | data formatting | bytes 2359296
  52.4 6.8 %convolution_add_fusion.5 = f32[192,4,384]{2,0,1:T(8,128)S(1)} fusion(f32[192,4,384]{2,0,1:T(8,128)} %convolution_bitcast_fusion.1, f32[192,3,384]{2,0,1:T(8,128)} %copy.198, f32[192,1,384]{2,0,1:T(8,128)S(1)} %copy-done.21, s32[384]{0:T(512)S(1)} %iota_add_fusion.2), kind=kOutput, calls=%fused_computation.23 | convolution fusion | flops 1363820544 | bytes 3540480 | tf_op jit(solution)/shard_map/xas,rs->xar/dot_general | solution.py:50
  59.3 6.3 %convolution_add_fusion.4 = f32[192,4,384]{2,0,1:T(8,128)} fusion(f32[192,4,384]{2,0,1:T(8,128)S(1)} %convolution_add_fusion.5, f32[192,2,384]{2,0,1:T(8,128)S(1)} %copy-done.18, f32[192,2,384]{2,0,1:T(8,128)S(1)} %copy-done.17, s32[384]{0:T(512)S(1)} %iota_add_fusion.1), kind=kOutput, calls=%fused_computation.22 | convolution fusion | flops 1363820544 | bytes 3540480 | tf_op jit(solution)/shard_map/xas,rs->xar/dot_general | solution.py:50
  66.2 12.0 %all-to-all-start = ((f32[32,1,9216]{2,1,0:T(1,128)}), f32[32,1,9216]{2,1,0:T(1,128)}, u32[]{:S(2)}, u32[]{:S(2)}) async-start(f32[32,1,9216]{2,1,0:T(1,128)} %reshape.479), calls=%async_computation | async-start | bytes 2359296 | tf_op jit(solution)/shard_map/all_to_all | solution.py:68
  78.7 5.7 %reduce.81 = f32[16,18432]{1,0:T(8,128)} reduce(f32[16,1,18432]{2,1,0:T(1,128)} %all-to-all-done.2, f32[]{:T(128)} %broadcast.929), dimensions={1}, to_apply=%all_to_all.68.reduce_sub_computation | reduce | bytes 2359300 | tf_op jit(solution)/shard_map/all_to_all | solution.py:73
  109.3 9.9 %all-to-all-start.3 = ((f32[4,16,48,96]{3,2,0,1:T(8,128)}), f32[4,16,48,96]{3,2,0,1:T(8,128)}, u32[]{:S(2)}, u32[]{:S(2)}) async-start(f32[4,16,48,96]{3,2,0,1:T(8,128)} %pad_maximum_fusion), calls=%async_computation.3 | async-start | bytes 3145728 | tf_op jit(solution)/shard_map/all_to_all | solution.py:76
  119.2 4.7 %reduce.82 = f32[32,9216]{1,0:T(8,128)S(1)} reduce(f32[32,1,9216]{2,1,0:T(1,128)} %all-to-all-done, f32[]{:T(128)} %broadcast.929), dimensions={1}, to_apply=%all_to_all.61.reduce_sub_computation | reduce | bytes 2359300 | tf_op jit(solution)/shard_map/all_to_all | solution.py:68
  139.1 6.0 %convolution_bitcast_fusion = f32[192,4,384]{2,0,1:T(8,128)} fusion(f32[192,4,384]{2,1,0:T(4,128)S(1)} %reshape.353), kind=kOutput, calls=%fused_computation.20 | convolution fusion | flops 1363230720 | bytes 2359296 | tf_op jit(solution)/shard_map/xas,rs->xar/dot_general | solution.py:50
  152.0 5.6 %convolution_add_fusion.2 = f32[192,4,384]{2,0,1:T(8,128)S(1)} fusion(f32[192,4,384]{2,0,1:T(8,128)S(1)} %copy-done.28, f32[192,3,384]{2,0,1:T(8,128)S(1)} %copy.204, f32[192,1,384]{2,0,1:T(8,128)S(1)} %copy.205, s32[384]{0:T(512)S(1)} %iota_add_fusion.2), kind=kOutput, calls=%fused_computation.19 | convolution fusion | flops 1363820544 | bytes 3540480 | tf_op jit(solution)/shard_map/xas,rs->xar/dot_general | solution.py:50
  157.7 5.2 %convolution_add_fusion.1 = f32[192,4,384]{2,0,1:T(8,128)S(1)} fusion(f32[192,4,384]{2,0,1:T(8,128)S(1)} %convolution_add_fusion.2, f32[192,2,384]{2,0,1:T(8,128)S(1)} %copy.206, f32[192,2,384]{2,0,1:T(8,128)S(1)} %copy.207, s32[384]{0:T(512)S(1)} %iota_add_fusion.1), kind=kOutput, calls=%fused_computation.18 | convolution fusion | flops 1363820544 | bytes 3540480 | tf_op jit(solution)/shard_map/xas,rs->xar/dot_general | solution.py:50
  162.9 5.3 %convolution_add_fusion = f32[192,4,384]{2,0,1:T(8,128)S(1)} fusion(f32[192,4,384]{2,0,1:T(8,128)S(1)} %convolution_add_fusion.1, f32[192,1,384]{2,0,1:T(8,128)S(1)} %copy.208, f32[192,3,384]{2,0,1:T(8,128)S(1)} %copy.209, s32[384]{0:T(512)S(1)} %iota_add_fusion), kind=kOutput, calls=%fused_computation.17 | convolution fusion | flops 1363820544 | bytes 3540480 | tf_op jit(solution)/shard_map/xas,rs->xar/dot_general | solution.py:50
  178.6 8.7 %all-to-all-start.1 = ((f32[32,1,9216]{2,1,0:T(1,128)}), f32[32,1,9216]{2,1,0:T(1,128)S(1)}, u32[]{:S(2)}, u32[]{:S(2)}) async-start(f32[32,1,9216]{2,1,0:T(1,128)} %reshape.481), calls=%async_computation.1 | async-start | bytes 2359296 | tf_op jit(solution)/shard_map/all_to_all | solution.py:71
  187.4 5.2 %convolution_add_fusion.3 = f32[192,4,384]{2,0,1:T(8,128)S(1)} fusion(f32[192,4,384]{2,0,1:T(8,128)S(1)} %copy-done.27, f32[192,1,384]{2,0,1:T(8,128)S(1)} %copy-done.20, f32[192,3,384]{2,0,1:T(8,128)S(1)} %copy-done.16, s32[384]{0:T(512)S(1)} %iota_add_fusion), kind=kOutput, calls=%fused_computation.21 | convolution fusion | flops 1363820544 | bytes 3540480 | tf_op jit(solution)/shard_map/xas,rs->xar/dot_general | solution.py:50
  202.9 14.9 %all-to-all-done.1 = f32[32,1,9216]{2,1,0:T(1,128)S(1)} async-done(((f32[32,1,9216]{2,1,0:T(1,128)}), f32[32,1,9216]{2,1,0:T(1,128)S(1)}, u32[]{:S(2)}, u32[]{:S(2)}) %all-to-all-start.1) | async-done | bytes 1179680 | tf_op jit(solution)/shard_map/all_to_all | solution.py:71
  221.2 4.6 %reshape.482 = f32[1536,1,4,48]{3,2,1,0:T(4,128)} reshape(f32[32,9216]{1,0:T(8,128)S(1)} %reduce.83) | data formatting | bytes 2359296
  239.4 7.2 %reduce.84 = f32[1536,48]{1,0:T(8,128)S(1)} reduce(f32[1536,1,48]{2,1,0:T(1,128)S(1)} %bitcast.138, f32[]{:T(128)} %broadcast.929), dimensions={1}, to_apply=%bitcast.116.reduce_sub_computation | reduce | bytes 589828
  248.1 9.8 %all-to-all-start.4 = ((f32[16,1,4608]{2,1,0:T(1,128)}), f32[16,1,4608]{2,1,0:T(1,128)S(1)}, u32[]{:S(2)}, u32[]{:S(2)}) async-start(f32[16,1,4608]{2,1,0:T(1,128)} %reshape.483), calls=%async_computation.4 | async-start | bytes 589824 | tf_op jit(solution)/shard_map/all_to_all | solution.py:79
  259.7 18.5 %copy.176 = f32[3,1,48,1536]{0,3,2,1:T(8,128)} copy(f32[3,1,48,1536]{3,2,0,1:T(8,128)S(1)} %slice_add_fusion) | data formatting | bytes 1769472 | tf_op jit(solution)/shard_map/add | solution.py:80
  278.2 39.5 %gather_fusion = f32[8192,3]{1,0:T(8,128)} fusion(f32[3,73728]{0,1:T(8,128)} %bitcast.121, s32[8192]{0:T(1024)S(1)} %broadcast_clamp_fusion), kind=kCustom, calls=%fused_computation | custom fusion | bytes 229376 | tf_op jit(solution)/shard_map/gather | solution.py:85
  317.7 8.1 %fusion.5 = f32[8192,3]{1,0:T(8,128)} fusion(f32[8192,3]{1,0:T(8,128)} %gather_fusion, f32[8192]{0:T(1024)S(1)} %copy-done.25, f32[1024,8]{1,0:T(8,128)S(1)} %copy-done.19), kind=kOutput, calls=%fused_computation.7 | output fusion | flops 52231 | bytes 262144 | tf_op jit(solution)/shard_map/mul | solution.py:87
  325.8 59.1 %scatter_custom_fusion = f32[3,73728]{0,1:T(8,128)} fusion(s32[8192]{0:T(1024)S(1)} %bitcast.146, f32[8192,3]{1,0:T(8,128)} %fusion.5, f32[]{:T(128)} %constant.341.clone.1), kind=kCustom, calls=%fused_computation.3 | custom fusion | flops 24576 | bytes 885248 | tf_op jit(solution)/shard_map/scatter-add | solution.py:88
  384.9 22.0 %copy.179 = f32[3,1,48,1536]{3,2,0,1:T(8,128)S(1)} copy(f32[3,1,48,1536]{0,3,2,1:T(8,128)} %bitcast.120) | data formatting | bytes 1769472 | tf_op jit(solution)/shard_map/reshape | solution.py:88
  (192 shorter events, 123.7 us)
Async XLA Ops:
  7.9 58.3 %all-to-all-start.2 = ((f32[16,1,18432]{2,1,0:T(1,128)}), f32[16,1,18432]{2,1,0:T(1,128)}, u32[]{:S(2)}, u32[]{:S(2)}) async-start(f32[16,1,18432]{2,1,0:T(1,128)} %reshape.477), calls=%async_computation.2 | async-start | bytes 2359296 | tf_op jit(solution)/shard_map/all_to_all | solution.py:73
  21.4 2.9 copy-start
  31.8 3.0 copy-start.24
  33.7 3.4 copy-start.22
  41.0 3.4 copy-start.7
  47.8 4.6 %copy-start.21 = (f32[192,1,384]{2,0,1:T(8,128)S(1)}, f32[192,1,384]{2,0,1:T(8,128)}, u32[]{:S(2)}) copy-start(f32[192,1,384]{2,0,1:T(8,128)} %copy.199) | copy-start | bytes 884740
  52.4 6.9 %copy-start.17 = (f32[192,2,384]{2,0,1:T(8,128)S(1)}, f32[192,2,384]{2,0,1:T(8,128)}, u32[]{:S(2)}) copy-start(f32[192,2,384]{2,0,1:T(8,128)} %copy.201) | copy-start | bytes 1769476
  52.4 6.9 %copy-start.18 = (f32[192,2,384]{2,0,1:T(8,128)S(1)}, f32[192,2,384]{2,0,1:T(8,128)}, u32[]{:S(2)}) copy-start(f32[192,2,384]{2,0,1:T(8,128)} %copy.200) | copy-start | bytes 1769476
  66.2 43.1 %all-to-all-start = ((f32[32,1,9216]{2,1,0:T(1,128)}), f32[32,1,9216]{2,1,0:T(1,128)}, u32[]{:S(2)}, u32[]{:S(2)}) async-start(f32[32,1,9216]{2,1,0:T(1,128)} %reshape.479), calls=%async_computation | async-start | bytes 2359296 | tf_op jit(solution)/shard_map/all_to_all | solution.py:68
  109.3 69.3 %all-to-all-start.3 = ((f32[4,16,48,96]{3,2,0,1:T(8,128)}), f32[4,16,48,96]{3,2,0,1:T(8,128)}, u32[]{:S(2)}, u32[]{:S(2)}) async-start(f32[4,16,48,96]{3,2,0,1:T(8,128)} %pad_maximum_fusion), calls=%async_computation.3 | async-start | bytes 3145728 | tf_op jit(solution)/shard_map/all_to_all | solution.py:76
  147.1 3.4 copy-start.13
  147.1 3.5 copy-start.10
  178.6 8.8 %copy-start.16 = (f32[192,3,384]{2,0,1:T(8,128)S(1)}, f32[192,3,384]{2,0,1:T(8,128)}, u32[]{:S(2)}) copy-start(f32[192,3,384]{2,0,1:T(8,128)} %copy.203) | copy-start | bytes 2654212
  178.6 8.8 %copy-start.20 = (f32[192,1,384]{2,0,1:T(8,128)S(1)}, f32[192,1,384]{2,0,1:T(8,128)}, u32[]{:S(2)}) copy-start(f32[192,1,384]{2,0,1:T(8,128)} %copy.202) | copy-start | bytes 884740
  178.6 8.8 %copy-start.27 = (f32[192,4,384]{2,0,1:T(8,128)S(1)}, f32[192,4,384]{2,0,1:T(8,128)}, u32[]{:S(2)}) copy-start(f32[192,4,384]{2,0,1:T(8,128)} %convolution_add_fusion.4) | copy-start | bytes 3538948
  178.6 39.1 %all-to-all-start.1 = ((f32[32,1,9216]{2,1,0:T(1,128)}), f32[32,1,9216]{2,1,0:T(1,128)S(1)}, u32[]{:S(2)}, u32[]{:S(2)}) async-start(f32[32,1,9216]{2,1,0:T(1,128)} %reshape.481), calls=%async_computation.1 | async-start | bytes 2359296 | tf_op jit(solution)/shard_map/all_to_all | solution.py:71
  197.4 2.7 copy-start.2
  234.6 3.0 copy-start.6
  239.4 18.6 %copy-start.3 = (f32[3,1,48,1536]{3,2,0,1:T(8,128)S(1)}, f32[3,1,48,1536]{3,2,0,1:T(8,128)}, u32[]{:S(2)}) copy-start(f32[3,1,48,1536]{3,2,0,1:T(8,128)} %copy-done.2) | copy-start | bytes 2654212
  246.6 11.3 %copy-start.1 = (f32[4,1,48,1536]{3,2,1,0:T(8,128)S(1)}, f32[4,1,48,1536]{3,2,1,0:T(8,128)}, u32[]{:S(2)}) copy-start(f32[4,1,48,1536]{3,2,1,0:T(8,128)} %param.14) | copy-start | bytes 3538948
  248.1 159.9 %all-to-all-start.4 = ((f32[16,1,4608]{2,1,0:T(1,128)}), f32[16,1,4608]{2,1,0:T(1,128)S(1)}, u32[]{:S(2)}, u32[]{:S(2)}) async-start(f32[16,1,4608]{2,1,0:T(1,128)} %reshape.483), calls=%async_computation.4 | async-start | bytes 589824 | tf_op jit(solution)/shard_map/all_to_all | solution.py:79
  278.2 39.5 %copy-start.19 = (f32[1024,8]{1,0:T(8,128)S(1)}, f32[1024,8]{1,0:T(8,128)}, u32[]{:S(2)}) copy-start(f32[1024,8]{1,0:T(8,128)} %copy.177) | copy-start | bytes 98308
  278.2 39.5 %copy-start.25 = (f32[8192]{0:T(1024)S(1)}, f32[8192]{0:T(1024)}, u32[]{:S(2)}) copy-start(f32[8192]{0:T(1024)} %mul.788) | copy-start | bytes 98308
  384.9 22.0 %copy-start.12 = (f32[6,8,12,128]{3,1,2,0:T(8,128)S(1)}, f32[6,8,12,128]{3,1,2,0:T(8,128)}, u32[]{:S(2)}) copy-start(f32[6,8,12,128]{3,1,2,0:T(8,128)} %copy.211) | copy-start | bytes 884740
  (10 other events, 14.2 us)
where the time goes:
time: 416 us; the launch traced here: 412 us
  local copies, waits for them, and re-layouts  187 us (45%)
  other arithmetic  111 us (27%)
  starting transfers between devices  51.3 us (12%)
  matrix products  46.5 us (11%)
  waiting for transfers between devices  14.9 us (4%)
    scatter-add x1, other arithmetic, body(): jnp.zeros_like(flattened).at[:, cells_index].add(spread).reshape(shaped)  59.1 us
    unnamed x98, local copies, waits for them, and re-layouts  47.5 us
    dot_general x8, matrix products, spectral_along(): jnp.einsum('xas,rs->xar', shifted, table_block, precision=lax.Precision.H...  46.5 us
    gather x1, local copies, waits for them, and re-layouts, body(): flattened[:, cells_index].reshape(3, weights.shape[0], weights.shape[1])  39.5 us
    reshape x1, local copies, waits for them, and re-layouts, body(): jnp.zeros_like(flattened).at[:, cells_index].add(spread).reshape(shaped)  22 us
    add x1, local copies, waits for them, and re-layouts, body(): provisional = flow_fields[:3] + 0.1 * tendency  18.5 us
    all_to_all x1, waiting for transfers between devices, body(): lax.all_to_all(returned, 'pen', split_axis=2, concat_axis=3, tiled=True)  14.9 us
    all_to_all x1, starting transfers between devices, body(): lax.all_to_all(flow_fields, 'pen', split_axis=3, concat_axis=2, tiled=True)  12 us
  transfers between devices with their start and end apart: 5, of which 1 were waited for; matrix products, arithmetic and copies ran while one was open for 72% of the time, Pallas kernels for 0%

commit v1 on v0

v1 whole, which is shorter than its diff:
```python
import math

import jax
import jax.numpy as jnp
import numpy as np
from jax import lax
from jax.experimental import pallas as pl
from jax.experimental.pallas import tpu as pltpu
from jax.sharding import PartitionSpec as P

MESH = pl.DeviceIdType.MESH
F32, BF16 = jnp.float32, jnp.bfloat16
NG, NP = 16, 32
ROWS, NZ, HALF = 48, 1536, 768
LANES, SPLIT, MK, ST = 128, 512, 1024, 8
PACK = ROWS + ROWS // 2


def bf16_parts(values):
    high = values.astype(BF16)
    return high, (values - high.astype(F32)).astype(BF16)


def table_rows():
    lag = np.arange(2 * HALF)
    safe = np.where(lag % HALF == 0, 1, lag)
    line = math.pi / NZ * (1 - 2 * (lag % 2)) / np.tan(math.pi * safe / NZ)
    line = np.where(lag % HALF == 0, 0.0, line)
    other = np.roll(line, -HALF)
    rows = []
    for values, width in ((0.5 * (line + other), HALF), (0.5 * (line - other), 2 * HALF)):
        where = (np.arange(16)[:, None] - np.arange(width)[None, :]) % (2 * HALF)
        block = values[where].astype(np.float32)
        high = block.astype(jnp.bfloat16).astype(np.float32)
        rows += [high, (block - high).astype(jnp.bfloat16).astype(np.float32)]
    return rows


def elimination():
    upper, scale, last = [], [], 0.0
    for _ in range(NG):
        pivot = 1.0 / (1.0 - last / 3.0)
        last = pivot / 3.0
        upper.append(last)
        scale.append(pivot)
    return upper, scale


def kernel(
    flow, cells, weights, solid, rah, ral, rbh, rbl,
    vel, pois,
    psend, precv, pmid, pback, grecv, gmid, gback, dsend, drecv,
    tah, tal, tbh, tbl, xsh, xsl, xdh, xdl, ysum, ydif, fsh, fsl, fdh, fdl,
    pre, div, prov, phi, plo, hot, corr, acc,
    ssem, rsem,
):
    me_g, me_p = lax.axis_index("grp"), lax.axis_index("pen")
    lane = lax.broadcasted_iota(jnp.int32, (ROWS // 2, LANES), 1) < LANES // 2
    dot = lambda a, b: jnp.dot(a, b, preferred_element_type=F32)

    barrier = pltpu.get_barrier_semaphore()

    def greet(axis, me, count):
        def step(d, carry):
            pl.semaphore_signal(
                barrier, 1, device_id={axis: lax.rem(me + d, count)}, device_id_type=MESH
            )
            return carry
        lax.fori_loop(1, count, step, 0)

    greet("pen", me_p, NP)
    greet("grp", me_g, NG)

    def push(axis, me, count, source, target, phase, whole=True):
        def step(d, carry):
            peer = lax.rem(me + d, count)
            if whole:
                src = source.at[peer]
            else:
                start = pl.multiple_of(lax.rem(peer, 4) * 384, 128)
                src = source.at[lax.div(peer, 4), :, pl.ds(start, 384)]
            pltpu.make_async_remote_copy(
                src_ref=src, dst_ref=target.at[me],
                send_sem=ssem.at[phase], recv_sem=rsem.at[phase],
                device_id={axis: peer}, device_id_type=MESH,
            ).start()
            return carry
        lax.fori_loop(1, count, step, 0)

    def arrived(target, count, phase):
        ref = target.at[pl.ds(0, count - 1)]
        pltpu.make_async_copy(ref, ref, rsem.at[phase]).wait()

    def sent(source, count, phase):
        ref = source.at[pl.ds(0, count - 1)]
        pltpu.make_async_copy(ref, ref, ssem.at[phase]).wait()

    for tile in range(NP):
        psend[tile, :ROWS, :] = flow[tile // 12, :, pl.ds(tile % 12 * LANES, LANES)]
    for j in range(NP // 2):
        tile = NP + j
        top = flow[tile // 12, :24, pl.ds(tile % 12 * LANES, LANES)]
        low = flow[tile // 12, 24:, pl.ds(tile % 12 * LANES, LANES)]
        psend[2 * j, ROWS:, :] = jnp.where(lane, top, pltpu.roll(low, 64, 1))
        psend[2 * j + 1, ROWS:, :] = jnp.where(lane, pltpu.roll(top, 64, 1), low)

    pl.semaphore_wait(barrier, NP - 1 + NG - 1)
    push("grp", me_g, NG, flow, grecv, 0, whole=False)
    push("pen", me_p, NP, psend, precv, 1)
    start = pl.multiple_of(lax.rem(me_g, 4) * 384, 128)
    grecv[me_g] = flow[lax.div(me_g, 4), :, pl.ds(start, 384)]
    precv[me_p] = psend[me_p]

    def fill(b, carry):
        rows = pl.ds(pl.multiple_of(b * 16, 16), 16)
        tah[rows, :] = pltpu.roll(rah[...], b * 16, 1).astype(BF16)
        tal[rows, :] = pltpu.roll(ral[...], b * 16, 1).astype(BF16)
        tbh[rows, :] = pltpu.roll(rbh[...], b * 16, 1)[:, :HALF].astype(BF16)
        tbl[rows, :] = pltpu.roll(rbl[...], b * 16, 1)[:, :HALF].astype(BF16)
        return carry
    lax.fori_loop(0, HALF // 16, fill, 0)

    for f in range(4):
        rows = pl.ds(f * ROWS, ROWS)
        one, two = flow[f, :, :HALF], flow[f, :, HALF:]
        xsh[rows, :], xsl[rows, :] = bf16_parts(one + two)
        xdh[rows, :], xdl[rows, :] = bf16_parts(one - two)

    def slopes(n, carry):
        cols = pl.ds(pl.multiple_of(n * 256, 256), 256)
        total = dot(xsh[...], tah[:, cols]) + dot(xsl[...], tah[:, cols]) + dot(xsh[...], tal[:, cols])
        other = dot(xdh[...], tbh[:, cols]) + dot(xdl[...], tbh[:, cols]) + dot(xdh[...], tbl[:, cols])
        for side, value in ((0, -(total + other)), (1, other - total)):
            where = pl.ds(pl.multiple_of(side * HALF + n * 256, 256), 256)
            along = flow[2, :, where]
            for i in range(3):
                slope = along * value[i * ROWS:(i + 1) * ROWS]
                if i == 2:
                    slope = slope + value[3 * ROWS:]
                pre[i, :, where] = flow[i, :, where] - 0.1 * slope
            div[:, where] = value[2 * ROWS:3 * ROWS]
        return carry
    lax.fori_loop(0, 3, slopes, 0)

    def places(s, carry):
        row = cells[pl.ds(s, 1), :] & (SPLIT - 1)
        def part(b, inner):
            index = lax.broadcasted_iota(jnp.int32, (16, MK), 0) + b * 16
            hot[s, pl.ds(pl.multiple_of(b * 16, 16), 16), :] = jnp.where(index == row, 1.0, 0.0).astype(BF16)
            return inner
        lax.fori_loop(0, SPLIT // 16, part, 0)
        return carry
    lax.fori_loop(0, ST, places, 0)

    upper, scale = elimination()
    arrived(grecv, NG, 0)

    def lines(t, carry):
        at = (pl.ds(pl.multiple_of(lax.div(t, 3) * 8, 8), 8), pl.ds(pl.multiple_of(lax.rem(t, 3) * LANES, LANES), LANES))
        f = [grecv[(i, *at)] for i in range(NG)]
        get = lambda i: f[i] if 0 <= i < NG else jnp.zeros_like(f[0])
        done = []
        for i in range(NG):
            value = (7.0 / 9.0) * (get(i + 1) - get(i - 1)) + (1.0 / 36.0) * (get(i + 2) - get(i - 2))
            if i:
                value = (value - done[-1] * (1.0 / 3.0)) * scale[i]
            done.append(value)
        value = done[-1]
        gmid[(NG - 1, *at)] = value
        for i in reversed(range(NG - 1)):
            value = done[i] - upper[i] * value
            gmid[(i, *at)] = value
        return carry
    lax.fori_loop(0, 18, lines, 0)
    push("grp", me_g, NG, gmid, gback, 2)
    gback[me_g] = gmid[me_g]

    arrived(precv, NP, 1)

    def halves(q, carry):
        rows = pl.ds(pl.multiple_of(q * ROWS, 16), ROWS)
        one, two = precv[q], precv[q + NP // 2]
        for high, low, value in ((fsh, fsl, one + two), (fdh, fdl, one - two)):
            packed = value[ROWS:]
            rest = jnp.concatenate([packed, pltpu.roll(packed, 64, 1)], axis=0)
            high[rows, :LANES], low[rows, :LANES] = bf16_parts(value[:ROWS])
            high[rows, LANES:], low[rows, LANES:] = bf16_parts(rest)
        return carry
    lax.fori_loop(0, NP // 2, halves, 0)

    def across(m, carry):
        rows = pl.ds(pl.multiple_of(m * 256, 256), 256)
        ysum[rows, :] = dot(tah[rows, :], fsh[...]) + dot(tah[rows, :], fsl[...]) + dot(tal[rows, :], fsh[...])
        ydif[rows, :] = dot(tbh[rows, :], fdh[...]) + dot(tbh[rows, :], fdl[...]) + dot(tbl[rows, :], fdh[...])
        return carry
    lax.fori_loop(0, 3, across, 0)

    def pieces(q, carry):
        rows = pl.ds(pl.multiple_of(q * ROWS, 8), ROWS)
        total, other = ysum[rows, :], ydif[rows, :]
        for slot, value in ((q, total + other), (q + NP // 2, total - other)):
            pmid[slot, :ROWS, :] = value[:, :LANES]
            rest = value[:, LANES:]
            pmid[slot, ROWS:, :] = jnp.where(lane, rest[:24], pltpu.roll(rest[24:], 64, 1))
        return carry
    lax.fori_loop(0, NP // 2, pieces, 0)
    push("pen", me_p, NP, pmid, pback, 3)
    pback[me_p] = pmid[me_p]

    arrived(gback, NG, 2)
    arrived(pback, NP, 3)
    for zt in range(12):
        cols = pl.ds(zt * LANES, LANES)
        d1 = []
        for f in range(4):
            tile = f * 12 + zt
            if tile < NP:
                d1.append(pback[tile, :ROWS, :])
            else:
                j = tile - NP
                one, two = pback[2 * j, ROWS:, :], pback[2 * j + 1, ROWS:, :]
                d1.append(jnp.concatenate([
                    jnp.where(lane, one, pltpu.roll(two, 64, 1)),
                    jnp.where(lane, pltpu.roll(one, 64, 1), two),
                ], axis=0))
        d0 = [gback[4 * f + zt // 3, :, pl.ds(zt % 3 * LANES, LANES)] for f in range(4)]
        u0, u1 = flow[0, :, cols], flow[1, :, cols]
        for i in range(3):
            slope = u0 * d0[i] + u1 * d1[i]
            if i == 0:
                slope = slope + d0[3]
            if i == 1:
                slope = slope + d1[3]
            value = pre[i, :, cols] - 0.1 * slope
            prov[i, :, cols] = value
            high, low = bf16_parts(value)
            rows = pl.ds((zt // 4 * 3 + i) * ROWS, ROWS)
            phi[rows, pl.ds(zt % 4 * LANES, LANES)] = high
            plo[rows, pl.ds(zt % 4 * LANES, LANES)] = low
        div[:, cols] = div[:, cols] + d0[0] + d1[1]

    wide = lax.broadcasted_iota(jnp.int32, (ROWS, LANES), 1)
    for g in range(NG):
        tile, off = divmod(96 * g, LANES)
        value = div[:, pl.ds(tile * LANES, LANES)]
        if off:
            value = pltpu.roll(value, LANES - off, 1)
        if off > 32:
            value = jnp.where(wide < LANES - off, value, pltpu.roll(div[:, pl.ds((tile + 1) * LANES, LANES)], LANES - off, 1))
        dsend[g] = value
    push("grp", me_g, NG, dsend, drecv, 4)
    drecv[me_g] = dsend[me_g]

    count = 3 * lax.broadcasted_iota(jnp.int32, (ROWS, MK), 0)
    acc[...] = jnp.zeros_like(acc)

    def sample(s, carry):
        place = hot[s]
        got = dot(phi[...], place) + dot(plo[...], place)
        code = cells[pl.ds(s, 1), :] >> 9
        weight = weights[pl.ds(s, 1), :]
        for i in range(3):
            total = None
            for zb in range(3):
                at = (zb * 3 + i) * ROWS
                picked = jnp.where(count + zb == code, got[at:at + ROWS], 0.0)
                picked = jnp.sum(picked.reshape(6, 8, MK), axis=0)
                total = picked if total is None else total + picked
            acc[i] += total * weight
        return carry
    lax.fori_loop(0, ST, sample, 0)
    sampled = [jnp.sum(acc[i], axis=0, keepdims=True) for i in range(3)]

    corr[...] = jnp.zeros_like(corr)

    def spread(s, carry):
        place = hot[s]
        code = cells[pl.ds(s, 1), :] >> 9
        weight = weights[pl.ds(s, 1), :]
        masks = [count + zb == code for zb in range(3)]
        parts = []
        for i in range(3):
            value = sampled[i] * weight
            high = value.astype(BF16).astype(F32)
            parts.append((high, (value - high).astype(BF16).astype(F32)))
        total = None
        for side in range(2):
            table = jnp.concatenate(
                [jnp.where(masks[zb], parts[i][side], 0.0).astype(BF16) for zb in range(3) for i in range(3)], axis=0
            )
            value = lax.dot_general(table, place, (((1,), (1,)), ((), ())), preferred_element_type=F32)
            total = value if total is None else total + value
        corr[...] += total
        return carry
    lax.fori_loop(0, ST, spread, 0)

    for zt in range(12):
        cols = pl.ds(zt * LANES, LANES)
        fluid = 1.0 - jnp.broadcast_to(solid[:, zt:zt + 1].astype(F32), (ROWS, LANES))
        for i in range(3):
            part = corr[pl.ds((zt // 4 * 3 + i) * ROWS, ROWS), pl.ds(zt % 4 * LANES, LANES)]
            vel[i, :, cols] = fluid * (prov[i, :, cols] - part)

    arrived(drecv, NG, 4)
    pois[...] = drecv[:, :, :96]

    sent(grecv, NG, 0)
    sent(psend, NP, 1)
    sent(gmid, NG, 2)
    sent(pmid, NP, 3)
    sent(dsend, NG, 4)


def body(flow_fields, marker_cells, marker_weights, solid_blocks):
    vmem = pl.BlockSpec(memory_space=pltpu.VMEM)
    tables = [jnp.asarray(rows) for rows in table_rows()]
    V = pltpu.VMEM
    velocity, source = pl.pallas_call(
        kernel,
        name="substep",
        out_shape=(
            jax.ShapeDtypeStruct((3, ROWS, NZ), F32),
            jax.ShapeDtypeStruct((NG, ROWS, 96), F32),
        ),
        in_specs=[vmem] * 8,
        out_specs=(vmem, vmem),
        scratch_shapes=[
            V((NP, PACK, LANES), F32), V((NP, PACK, LANES), F32), V((NP, PACK, LANES), F32), V((NP, PACK, LANES), F32),
            V((NG, ROWS, 384), F32), V((NG, ROWS, 384), F32), V((NG, ROWS, 384), F32),
            V((NG, ROWS, LANES), F32), V((NG, ROWS, LANES), F32),
            V((HALF, HALF), BF16), V((HALF, HALF), BF16), V((HALF, HALF), BF16), V((HALF, HALF), BF16),
            V((4 * ROWS, HALF), BF16), V((4 * ROWS, HALF), BF16), V((4 * ROWS, HALF), BF16), V((4 * ROWS, HALF), BF16),
            V((HALF, 256), F32), V((HALF, 256), F32),
            V((HALF, 256), BF16), V((HALF, 256), BF16), V((HALF, 256), BF16), V((HALF, 256), BF16),
            V((3, ROWS, NZ), F32), V((ROWS, NZ), F32), V((3, ROWS, NZ), F32),
            V((9 * ROWS, SPLIT), BF16), V((9 * ROWS, SPLIT), BF16),
            V((ST, SPLIT, MK), BF16), V((9 * ROWS, SPLIT), F32), V((3, 8, MK), F32),
            pltpu.SemaphoreType.DMA((5,)), pltpu.SemaphoreType.DMA((5,)),
        ],
        compiler_params=pltpu.CompilerParams(
            collective_id=0, has_side_effects=True, vmem_limit_bytes=60 * 1024 * 1024
        ),
    )(
        flow_fields.reshape(4, ROWS, NZ),
        marker_cells[0, 0].T,
        marker_weights[0, 0].T,
        solid_blocks[0],
        *tables,
    )
    return velocity.reshape(3, 1, ROWS, NZ), source


def solution(mesh):
    return jax.shard_map(
        body,
        mesh=mesh,
        in_specs=(
            P(None, "grp", "pen", None),
            P("grp", "pen", None, None),
            P("grp", "pen", None, None),
            P("grp", "pen", None),
        ),
        out_specs=(P(None, "grp", "pen", None), P(None, "pen", "grp")),
        check_vma=False,
    )
```

time: 416 us -> 136 us (0.33)
  local copies, waits for them, and re-layouts: 187 us -> 4.32 us
  Pallas kernels: 0 us -> 129 us
  other arithmetic: 111 us -> 0 us
  starting transfers between devices: 51.3 us -> 0 us
  matrix products: 46.5 us -> 0 us
  waiting for transfers between devices: 14.9 us -> 0 us
    pallas_call x0 -> x1, Pallas kernels: none -> 129 us  [body(): pl.pallas_call(kernel, name='substep', out_shape=(jax.ShapeDtypeStruct((3...]
    scatter-add x4 -> x0, other arithmetic: 59.5 us -> none  [the longest x1 59.1 us: body(): jnp.zeros_like(flattened).at[:, cells_index].add(spread).reshape(shaped)]
    all_to_all x5 -> x0, starting transfers between devices: 51.3 us -> none  [the longest x1 12 us: body(): lax.all_to_all(flow_fields, 'pen', split_axis=3, concat_axis=2, tiled=True)]
    dot_general x8 -> x0, matrix products: 46.5 us -> none  [spectral_along(): jnp.einsum('xas,rs->xar', shifted, table_block, precision=lax.Precision.H...]
    unnamed x98 -> x5, local copies, waits for them, and re-layouts: 47.5 us -> 4.32 us
    gather x1 -> x0, local copies, waits for them, and re-layouts: 39.5 us -> none  [body(): flattened[:, cells_index].reshape(3, weights.shape[0], weights.shape[1])]
    reshape x5 -> x0, local copies, waits for them, and re-layouts: 29.3 us -> none  [the longest x1 22 us: body(): jnp.zeros_like(flattened).at[:, cells_index].add(spread).reshape(shaped)]
    slice x20 -> x0, local copies, waits for them, and re-layouts: 24.2 us -> none  [the longest x6 9.52 us: spectral_along(): shifted = jnp.roll(line_blocks, lag_block, axis=1)]
  transfers between devices with their start and end apart: 5 -> 0, of which waited for: 1 -> 0; matrix products, arithmetic and copies ran while one was open for 72% -> 0% of each run, Pallas kernels for 0% -> 0%
where the time goes in v1:
time: 136 us; the launch traced here: 134 us
  Pallas kernels  129 us (95%)
  local copies, waits for them, and re-layouts  4.32 us (3%)
    pallas_call x1, Pallas kernels, body(): pl.pallas_call(kernel, name='substep', out_shape=(jax.ShapeDtypeStruct((3...  129 us
    unnamed x5, local copies, waits for them, and re-layouts  4.32 us

profile of v1, /device:TPU:1, one launch (start us, length us, event | category | flops | bytes accessed | tf_op | source)
XLA Modules:
  0.0 133.9 jit_solution(1128212706881531411)
XLA Ops:
  0.6 1.4 %copy.10 = s32[1,48,12]{2,1,0:T(8,128)} copy(s32[1,48,12]{1,0,2:T(1,128)} %param.11) | data formatting | bytes 4608 | tf_op args[3]
  2.0 128.9 %substep.1 = (f32[3,48,1536]{2,1,0:T(8,128)}, f32[16,48,96]{2,1,0:T(8,128)}) custom-call(f32[4,48,1536]{2,1,0:T(8,128)} %bitcast.11, s32[8,1024]{1,0:T(8,128)} %bitcast.14, f32[8,1024]{1,0:T(8,128)} %bitcast.15, s32[48,12]{1,0:T(8,128)} %bitcast.13, f32[16,768]{1,0:T(8,128)} %constant.8.clone.rah, f32[16,768]{1,0:T(8,128)} %constant.9.clone.ral, ...), custom_call_target="tpu_custom_call" | custom-call | tf_op jit(solution)/shard_map/substep/pallas_call | solution.py:318
  130.9 0.0 copy-start
  130.9 2.2 %copy.14 = f32[3,1,48,1536]{3,2,1,0:T(8,128)} copy(f32[3,1,48,1536]{3,2,1,0:T(8,128)} %bitcast.12) | data formatting | bytes 1769472
  133.1 0.0 copy-done
  133.1 0.7 copy.15
Async XLA Ops:
  130.9 2.2 %copy-start = (f32[16,48,96]{2,1,0:T(8,128)S(1)}, f32[16,48,96]{2,1,0:T(8,128)}, u32[]{:S(2)}) copy-start(f32[16,48,96]{2,1,0:T(8,128)} %get-tuple-element.11) | copy-start | bytes 884740

commit v2 on v1

v2 whole, which is shorter than its diff:
```python
import math

import jax
import jax.numpy as jnp
import numpy as np
from jax import lax
from jax.experimental import pallas as pl
from jax.experimental.pallas import tpu as pltpu
from jax.sharding import PartitionSpec as P

MESH = pl.DeviceIdType.MESH
F32, BF16 = jnp.float32, jnp.bfloat16
NG, NP = 16, 32
ROWS, NZ, HALF = 48, 1536, 768
LANES, SPLIT, MK, ST = 128, 512, 1024, 8
PARTS = NZ // SPLIT


def bf16_parts(values):
    high = values.astype(BF16)
    return high, (values - high.astype(F32)).astype(BF16)


def table_rows():
    lag = np.arange(2 * HALF)
    safe = np.where(lag % HALF == 0, 1, lag)
    line = math.pi / NZ * (1 - 2 * (lag % 2)) / np.tan(math.pi * safe / NZ)
    line = np.where(lag % HALF == 0, 0.0, line)
    other = np.roll(line, -HALF)
    rows = []
    for values, width in ((0.5 * (line + other), HALF), (0.5 * (line - other), 2 * HALF)):
        where = (np.arange(16)[:, None] - np.arange(width)[None, :]) % (2 * HALF)
        block = values[where].astype(np.float32)
        high = block.astype(jnp.bfloat16).astype(np.float32)
        rows += [high, (block - high).astype(jnp.bfloat16).astype(np.float32)]
    return rows


def elimination():
    upper, scale, last = [], [], 0.0
    for _ in range(NG):
        pivot = 1.0 / (1.0 - last / 3.0)
        last = pivot / 3.0
        upper.append(last)
        scale.append(pivot)
    return upper, scale


def kernel(
    flow, cells, weights, solid, rah, ral, rbh, rbl,
    vel, pois,
    psend, precv, pmid, pback, grecv, gmid, gback, dsend, drecv,
    tah, tal, tbh, tbl, xsh, xsl, xdh, xdl, ysum, ydif, fsum, fdif,
    pre, div, prov, phi, plo, hot, corr, acc, fluid,
    ssem, rsem,
):
    me_g, me_p = lax.axis_index("grp"), lax.axis_index("pen")
    lane = lax.broadcasted_iota(jnp.int32, (ROWS // 2, LANES), 1) < LANES // 2
    wide = lax.broadcasted_iota(jnp.int32, (ROWS, LANES), 1)
    dot = lambda a, b: jnp.dot(a, b, preferred_element_type=F32)
    swap = lambda value: pltpu.roll(value, LANES // 2, 1)
    barrier = pltpu.get_barrier_semaphore()

    def nth(k, middle, size):
        return lax.rem(middle + (1 - 2 * lax.rem(k, 2)) * lax.div(k + 1, 2), size)

    def pen_peer(t):
        z = lax.rem(lax.div(me_p, 2) + nth(lax.div(t, 4), 4, 8), 8)
        y = lax.rem(lax.div(me_p, 16) + 1 + lax.div(t, 2), 2)
        return y * 16 + z * 2 + lax.rem(me_p + t, 2)

    def grp_peer(t):
        x = lax.rem(me_g + nth(lax.div(t, 4), 2, 4), 4)
        y = lax.rem(lax.div(me_g, 4) + nth(lax.rem(t, 4), 2, 4), 4)
        return y * 4 + x

    def greet(axis, me, count):
        def step(d, carry):
            pl.semaphore_signal(
                barrier, 1, device_id={axis: lax.rem(me + d, count)}, device_id_type=MESH
            )
            return carry
        lax.fori_loop(1, count, step, 0)

    def push(axis, peer, src, dst, phase):
        pltpu.make_async_remote_copy(
            src_ref=src, dst_ref=dst, send_sem=ssem.at[phase], recv_sem=rsem.at[phase],
            device_id={axis: peer}, device_id_type=MESH,
        ).start()

    def exchange(to_pen, to_grp):
        def step(t, carry):
            to_pen(pen_peer(2 * t))
            to_pen(pen_peer(2 * t + 1))
            to_grp(grp_peer(t))
            return carry
        lax.fori_loop(0, NG - 1, step, 0)
        to_pen(pen_peer(NP - 1))

    def arrived(target, count, phase):
        ref = target.at[pl.ds(0, count - 1)]
        pltpu.make_async_copy(ref, ref, rsem.at[phase]).wait()

    def sent(source, count, phase):
        ref = source.at[pl.ds(0, count - 1)]
        pltpu.make_async_copy(ref, ref, ssem.at[phase]).wait()

    def mine(c, i):
        return flow.at[lax.div(i, 4), :, pl.ds(pl.multiple_of((lax.rem(i, 4) + 4 * c) * LANES, LANES), LANES)]

    greet("pen", me_p, NP)
    greet("grp", me_g, NG)

    for c in range(PARTS):
        for tile in range(16):
            cols = pl.ds((4 * c + tile % 4) * LANES, LANES)
            top, low = flow[tile // 4, :24, cols], flow[tile // 4, 24:, cols]
            psend[c, 2 * tile] = jnp.where(lane, top, swap(low))
            psend[c, 2 * tile + 1] = jnp.where(lane, swap(top), low)

    pl.semaphore_wait(barrier, NP - 1 + NG - 1)
    for c in range(PARTS):
        exchange(
            lambda peer: push("pen", peer, psend.at[c, peer], precv.at[c, me_p], c),
            lambda peer: push("grp", peer, mine(c, peer), grecv.at[c, me_g], PARTS + c),
        )
    for c in range(PARTS):
        precv[c, me_p] = psend[c, me_p]
        grecv[c, me_g] = mine(c, me_g)[...]

    def fill(b, carry):
        rows = pl.ds(pl.multiple_of(b * 16, 16), 16)
        tah[rows, :] = pltpu.roll(rah[...], b * 16, 1).astype(BF16)
        tal[rows, :] = pltpu.roll(ral[...], b * 16, 1).astype(BF16)
        tbh[rows, :] = pltpu.roll(rbh[...], b * 16, 1)[:, :HALF].astype(BF16)
        tbl[rows, :] = pltpu.roll(rbl[...], b * 16, 1)[:, :HALF].astype(BF16)
        return carry
    lax.fori_loop(0, HALF // 16, fill, 0)

    for f in range(4):
        rows = pl.ds(f * ROWS, ROWS)
        one, two = flow[f, :, :HALF], flow[f, :, HALF:]
        xsh[rows, :], xsl[rows, :] = bf16_parts(one + two)
        xdh[rows, :], xdl[rows, :] = bf16_parts(one - two)

    def slopes(n, carry):
        cols = pl.ds(pl.multiple_of(n * 256, 256), 256)
        total = dot(xsh[...], tah[:, cols]) + dot(xsl[...], tah[:, cols]) + dot(xsh[...], tal[:, cols])
        other = dot(xdh[...], tbh[:, cols]) + dot(xdl[...], tbh[:, cols]) + dot(xdh[...], tbl[:, cols])
        for side, value in ((0, -(total + other)), (1, other - total)):
            where = pl.ds(pl.multiple_of(side * HALF + n * 256, 256), 256)
            along = flow[2, :, where]
            for i in range(3):
                slope = along * value[i * ROWS:(i + 1) * ROWS]
                if i == 2:
                    slope = slope + value[3 * ROWS:]
                pre[i, :, where] = flow[i, :, where] - 0.1 * slope
            div[:, where] = value[2 * ROWS:3 * ROWS]
        return carry
    lax.fori_loop(0, 3, slopes, 0)

    def places(s, carry):
        row = cells[pl.ds(s, 1), :] & (SPLIT - 1)
        def part(b, inner):
            index = lax.broadcasted_iota(jnp.int32, (16, MK), 0) + b * 16
            hot[s, pl.ds(pl.multiple_of(b * 16, 16), 16), :] = jnp.where(index == row, 1.0, 0.0).astype(BF16)
            return inner
        lax.fori_loop(0, SPLIT // 16, part, 0)
        return carry
    lax.fori_loop(0, ST, places, 0)

    square = lax.broadcasted_iota(jnp.int32, (ROWS, ROWS), 0) == lax.broadcasted_iota(jnp.int32, (ROWS, ROWS), 1)
    for zt in range(12):
        open_cells = jnp.where(square, 1.0 - solid[zt].astype(F32), 0.0).astype(BF16)
        fluid[:, pl.ds(zt * LANES, LANES)] = dot(open_cells, jnp.ones((ROWS, LANES), BF16))

    upper, scale = elimination()
    for c in range(PARTS):
        arrived(grecv.at[c], NG, PARTS + c)

        def lines(t, carry):
            rows = pl.ds(pl.multiple_of(t * 8, 8), 8)
            f = [grecv[c, i, rows, :] for i in range(NG)]
            get = lambda i: f[i] if 0 <= i < NG else jnp.zeros_like(f[0])
            done = []
            for i in range(NG):
                value = (7.0 / 9.0) * (get(i + 1) - get(i - 1)) + (1.0 / 36.0) * (get(i + 2) - get(i - 2))
                if i:
                    value = (value - done[-1] * (1.0 / 3.0)) * scale[i]
                done.append(value)
            value = done[-1]
            gmid[c, NG - 1, rows, :] = value
            for i in reversed(range(NG - 1)):
                value = done[i] - upper[i] * value
                gmid[c, i, rows, :] = value
            return carry
        lax.fori_loop(0, ROWS // 8, lines, 0)
        gback[c, me_g] = gmid[c, me_g]

        arrived(precv.at[c], NP, c)

        def halves(q, carry):
            rows = pl.ds(pl.multiple_of(q * ROWS, 16), ROWS)
            one, two = precv[c, q], precv[c, q + NP // 2]
            for both, packed in ((fsum, one + two), (fdif, one - two)):
                value = jnp.concatenate([packed, swap(packed)], axis=0)
                high = value.astype(BF16).astype(F32)
                both[rows, :] = jnp.where(wide < LANES // 2, high, swap(value - high)).astype(BF16)
            return carry
        lax.fori_loop(0, NP // 2, halves, 0)

        def across(m, carry):
            rows = pl.ds(pl.multiple_of(m * 256, 256), 256)
            for out, high, low, both in ((ysum, tah, tal, fsum), (ydif, tbh, tbl, fdif)):
                value = dot(high[rows, :], both[...])
                out[rows, :] = value + swap(value) + dot(low[rows, :], both[...])
            return carry
        lax.fori_loop(0, 3, across, 0)

        def pieces(q, carry):
            rows = pl.ds(pl.multiple_of(q * ROWS, 8), ROWS)
            total, other = ysum[rows, :], ydif[rows, :]
            for slot, value in ((q, total + other), (q + NP // 2, total - other)):
                pmid[c, slot] = jnp.where(lane, value[:24], swap(value[24:]))
            return carry
        lax.fori_loop(0, NP // 2, pieces, 0)
        exchange(
            lambda peer: push("pen", peer, pmid.at[c, peer], pback.at[c, me_p], 2 * PARTS + c),
            lambda peer: push("grp", peer, gmid.at[c, peer], gback.at[c, me_g], 3 * PARTS + c),
        )
        pback[c, me_p] = pmid[c, me_p]

    count = 3 * lax.broadcasted_iota(jnp.int32, (ROWS, MK), 0)
    acc[...] = jnp.zeros_like(acc)
    corr[...] = jnp.zeros_like(corr)
    for c in range(PARTS):
        arrived(gback.at[c], NG, 3 * PARTS + c)
        arrived(pback.at[c], NP, 2 * PARTS + c)
        for k in range(4):
            cols = pl.ds((4 * c + k) * LANES, LANES)
            d0 = [gback[c, 4 * f + k] for f in range(4)]
            d1 = []
            for f in range(4):
                one, two = pback[c, 8 * f + 2 * k], pback[c, 8 * f + 2 * k + 1]
                d1.append(jnp.concatenate([jnp.where(lane, one, swap(two)), jnp.where(lane, swap(one), two)], axis=0))
            u0, u1 = flow[0, :, cols], flow[1, :, cols]
            for i in range(3):
                slope = u0 * d0[i] + u1 * d1[i]
                if i == 0:
                    slope = slope + d0[3]
                if i == 1:
                    slope = slope + d1[3]
                value = pre[i, :, cols] - 0.1 * slope
                prov[i, :, cols] = value
                rows = pl.ds((3 * c + i) * ROWS, ROWS)
                phi[rows, pl.ds(k * LANES, LANES)], plo[rows, pl.ds(k * LANES, LANES)] = bf16_parts(value)
            div[:, cols] = div[:, cols] + d0[0] + d1[1]

        if c == PARTS - 1:
            for g in range(NG):
                tile, off = divmod(96 * g, LANES)
                value = div[:, pl.ds(tile * LANES, LANES)]
                if off:
                    value = pltpu.roll(value, LANES - off, 1)
                if off > 32:
                    rest = pltpu.roll(div[:, pl.ds((tile + 1) * LANES, LANES)], LANES - off, 1)
                    value = jnp.where(wide < LANES - off, value, rest)
                dsend[g] = value

            def spread_out(t, carry):
                peer = grp_peer(t)
                push("grp", peer, dsend.at[peer], drecv.at[me_g], 4 * PARTS)
                return carry
            lax.fori_loop(0, NG - 1, spread_out, 0)
            drecv[me_g] = dsend[me_g]

        def sample(s, carry):
            place = hot[s]
            rows = pl.ds(3 * c * ROWS, 3 * ROWS)
            got = dot(phi[rows, :], place) + dot(plo[rows, :], place)
            mask = count + c == cells[pl.ds(s, 1), :] >> 9
            weight = weights[pl.ds(s, 1), :]
            for i in range(3):
                picked = jnp.where(mask, got[i * ROWS:(i + 1) * ROWS], 0.0)
                acc[i] += jnp.sum(picked.reshape(6, 8, MK), axis=0) * weight
            return carry
        lax.fori_loop(0, ST, sample, 0)

    sampled = [jnp.sum(acc[i], axis=0, keepdims=True) for i in range(3)]

    def spread(s, carry):
        place = hot[s]
        code = cells[pl.ds(s, 1), :] >> 9
        weight = weights[pl.ds(s, 1), :]
        masks = [count + zb == code for zb in range(3)]
        parts = []
        for i in range(3):
            value = sampled[i] * weight
            high = value.astype(BF16).astype(F32)
            parts.append((high, (value - high).astype(BF16).astype(F32)))
        total = None
        for side in range(2):
            table = jnp.concatenate(
                [jnp.where(masks[zb], parts[i][side], 0.0).astype(BF16) for zb in range(3) for i in range(3)], axis=0
            )
            value = lax.dot_general(table, place, (((1,), (1,)), ((), ())), preferred_element_type=F32)
            total = value if total is None else total + value
        corr[...] += total
        return carry
    lax.fori_loop(0, ST, spread, 0)

    for zt in range(12):
        cols = pl.ds(zt * LANES, LANES)
        for i in range(3):
            part = corr[pl.ds((zt // 4 * 3 + i) * ROWS, ROWS), pl.ds(zt % 4 * LANES, LANES)]
            vel[i, :, cols] = fluid[:, cols] * (prov[i, :, cols] - part)

    arrived(drecv, NG, 4 * PARTS)
    pois[...] = drecv[:, :, :96]

    for c in range(PARTS):
        sent(psend.at[c], NP, c)
        sent(grecv.at[c], NG, PARTS + c)
        sent(pmid.at[c], NP, 2 * PARTS + c)
        sent(gmid.at[c], NG, 3 * PARTS + c)
    sent(dsend, NG, 4 * PARTS)


def body(flow_fields, marker_cells, marker_weights, solid_blocks):
    vmem = pl.BlockSpec(memory_space=pltpu.VMEM)
    tables = [jnp.asarray(rows) for rows in table_rows()]
    V = pltpu.VMEM
    velocity, source = pl.pallas_call(
        kernel,
        name="substep",
        out_shape=(
            jax.ShapeDtypeStruct((3, ROWS, NZ), F32),
            jax.ShapeDtypeStruct((NG, ROWS, 96), F32),
        ),
        in_specs=[vmem] * 8,
        out_specs=(vmem, vmem),
        scratch_shapes=[
            *[V((PARTS, NP, ROWS // 2, LANES), F32)] * 4,
            *[V((PARTS, NG, ROWS, LANES), F32)] * 3,
            V((NG, ROWS, LANES), F32), V((NG, ROWS, LANES), F32),
            V((HALF, HALF), BF16), V((HALF, HALF), BF16), V((HALF, HALF), BF16), V((HALF, HALF), BF16),
            V((4 * ROWS, HALF), BF16), V((4 * ROWS, HALF), BF16), V((4 * ROWS, HALF), BF16), V((4 * ROWS, HALF), BF16),
            V((HALF, LANES), F32), V((HALF, LANES), F32), V((HALF, LANES), BF16), V((HALF, LANES), BF16),
            V((3, ROWS, NZ), F32), V((ROWS, NZ), F32), V((3, ROWS, NZ), F32),
            V((9 * ROWS, SPLIT), BF16), V((9 * ROWS, SPLIT), BF16),
            V((ST, SPLIT, MK), BF16), V((9 * ROWS, SPLIT), F32), V((3, 8, MK), F32), V((ROWS, NZ), F32),
            pltpu.SemaphoreType.DMA((4 * PARTS + 1,)), pltpu.SemaphoreType.DMA((4 * PARTS + 1,)),
        ],
        compiler_params=pltpu.CompilerParams(
            collective_id=0, has_side_effects=True, vmem_limit_bytes=60 * 1024 * 1024
        ),
    )(
        flow_fields.reshape(4, ROWS, NZ),
        marker_cells[0, 0].T,
        marker_weights[0, 0].T,
        solid_blocks.transpose(2, 0, 1),
        *tables,
    )
    return velocity.reshape(3, 1, ROWS, NZ), source


def solution(mesh):
    return jax.shard_map(
        body,
        mesh=mesh,
        in_specs=(
            P(None, "grp", "pen", None),
            P("grp", "pen", None, None),
            P("grp", "pen", None, None),
            P("grp", "pen", None),
        ),
        out_specs=(P(None, "grp", "pen", None), P(None, "pen", "grp")),
        check_vma=False,
    )
```

time: 136 us -> 113 us (0.83); the launches traced: 134 us -> 113 us
  Pallas kernels: 129 us -> 109 us
  local copies, waits for them, and re-layouts: 4.32 us -> 2.94 us
    pallas_call x1, Pallas kernels: 129 us -> 109 us  [body(): pl.pallas_call(kernel, name='substep', out_shape=(jax.ShapeDtypeStruct((3...]
    unnamed x5 -> x4, local copies, waits for them, and re-layouts: 4.32 us -> 2.94 us
where the time goes in v2:
time: 113 us
  Pallas kernels  109 us (96%)
  local copies, waits for them, and re-layouts  2.94 us (3%)
    pallas_call x1, Pallas kernels, body(): pl.pallas_call(kernel, name='substep', out_shape=(jax.ShapeDtypeStruct((3...  109 us
    unnamed x4, local copies, waits for them, and re-layouts  2.94 us

profile of v2, /device:TPU:1, one launch (start us, length us, event | category | flops | bytes accessed | tf_op | source)
XLA Modules:
  0.0 112.8 jit_solution(7646660792822521785)
XLA Ops:
  0.6 109.2 %substep.1 = (f32[3,48,1536]{2,1,0:T(8,128)}, f32[16,48,96]{2,1,0:T(8,128)}) custom-call(f32[4,48,1536]{2,1,0:T(8,128)} %bitcast.11, s32[8,1024]{1,0:T(8,128)} %bitcast.13, f32[8,1024]{1,0:T(8,128)} %bitcast.14, s32[12,1,48]{2,1,0:T(1,128)} %bitcast.15, f32[16,768]{1,0:T(8,128)} %constant.8.clone.rah, f32[16,768]{1,0:T(8,128)} %constant.9.clone.ral, ...), custom_call_target="tpu_custom_call" | custom-call | tf_op jit(solution)/shard_map/substep/pallas_call | solution.py:333
  109.9 0.0 copy-start
  109.9 2.2 %copy.13 = f32[3,1,48,1536]{3,2,1,0:T(8,128)} copy(f32[3,1,48,1536]{3,2,1,0:T(8,128)} %bitcast.12) | data formatting | bytes 1769472
  112.1 0.0 copy-done
  112.1 0.7 copy.14
Async XLA Ops:
  109.9 2.2 %copy-start = (f32[16,48,96]{2,1,0:T(8,128)S(1)}, f32[16,48,96]{2,1,0:T(8,128)}, u32[]{:S(2)}) copy-start(f32[16,48,96]{2,1,0:T(8,128)} %get-tuple-element.11) | copy-start | bytes 884740

commit v3 on v2

--- a/solution.py
+++ b/solution.py
@@ -47,12 +47,12 @@
 
 
 def kernel(
-    flow, cells, weights, solid, rah, ral, rbh, rbl,
+    source, cells, weights, solid, rah, ral, rbh, rbl,
     vel, pois,
-    psend, precv, pmid, pback, grecv, gmid, gback, dsend, drecv,
+    flow, psend, precv, pmid, pback, grecv, gmid, gback, dsend, drecv,
     tah, tal, tbh, tbl, xsh, xsl, xdh, xdl, ysum, ydif, fsum, fdif,
     pre, div, prov, phi, plo, hot, corr, acc, fluid,
-    ssem, rsem,
+    ssem, rsem, fsem,
 ):
     me_g, me_p = lax.axis_index("grp"), lax.axis_index("pen")
     lane = lax.broadcasted_iota(jnp.int32, (ROWS // 2, LANES), 1) < LANES // 2
@@ -108,8 +108,11 @@
     def mine(c, i):
         return flow.at[lax.div(i, 4), :, pl.ds(pl.multiple_of((lax.rem(i, 4) + 4 * c) * LANES, LANES), LANES)]
 
+    fetch = pltpu.make_async_copy(source, flow, fsem)
+    fetch.start()
     greet("pen", me_p, NP)
     greet("grp", me_g, NG)
+    fetch.wait()
 
     for c in range(PARTS):
         for tile in range(16):
@@ -334,12 +337,13 @@
         kernel,
         name="substep",
         out_shape=(
-            jax.ShapeDtypeStruct((3, ROWS, NZ), F32),
-            jax.ShapeDtypeStruct((NG, ROWS, 96), F32),
+            pltpu.VMEM((3, ROWS, NZ), F32),
+            pltpu.VMEM((NG, ROWS, 96), F32),
         ),
-        in_specs=[vmem] * 8,
+        in_specs=[pl.BlockSpec(memory_space=pl.ANY)] + [vmem] * 7,
         out_specs=(vmem, vmem),
         scratch_shapes=[
+            V((4, ROWS, NZ), F32),
             *[V((PARTS, NP, ROWS // 2, LANES), F32)] * 4,
             *[V((PARTS, NG, ROWS, LANES), F32)] * 3,
             V((NG, ROWS, LANES), F32), V((NG, ROWS, LANES), F32),
@@ -350,6 +354,7 @@
             V((9 * ROWS, SPLIT), BF16), V((9 * ROWS, SPLIT), BF16),
             V((ST, SPLIT, MK), BF16), V((9 * ROWS, SPLIT), F32), V((3, 8, MK), F32), V((ROWS, NZ), F32),
             pltpu.SemaphoreType.DMA((4 * PARTS + 1,)), pltpu.SemaphoreType.DMA((4 * PARTS + 1,)),
+            pltpu.SemaphoreType.DMA,
         ],
         compiler_params=pltpu.CompilerParams(
             collective_id=0, has_side_effects=True, vmem_limit_bytes=60 * 1024 * 1024

time: 113 us -> 110 us (0.973)
  local copies, waits for them, and re-layouts: 2.94 us -> 1.66 us
    pallas_call x1, Pallas kernels: 109 us -> 108 us  [body(): pl.pallas_call(kernel, name='substep', out_shape=(pltpu.VMEM((3, ROWS, NZ...]
    unnamed x4 -> x2, local copies, waits for them, and re-layouts: 2.94 us -> 1.66 us
where the time goes in v3:
time: 110 us
  Pallas kernels  108 us (98%)
  local copies, waits for them, and re-layouts  1.66 us (2%)
    pallas_call x1, Pallas kernels, body(): pl.pallas_call(kernel, name='substep', out_shape=(pltpu.VMEM((3, ROWS, NZ...  108 us

profile of v3, /device:TPU:1, one launch (start us, length us, event | category | flops | bytes accessed | tf_op | source)
XLA Modules:
  0.0 110.1 jit_solution(1016338406884439563)
XLA Ops:
  0.6 107.8 %substep.1 = (f32[3,48,1536]{2,1,0:T(8,128)S(1)}, f32[16,48,96]{2,1,0:T(8,128)S(1)}) custom-call(f32[4,48,1536]{2,1,0:T(8,128)} %bitcast.12, s32[8,1024]{1,0:T(8,128)} %bitcast.13, f32[8,1024]{1,0:T(8,128)} %bitcast.14, s32[12,1,48]{2,1,0:T(1,128)} %bitcast.15, f32[16,768]{1,0:T(8,128)} %constant.8.clone.rah, f32[16,768]{1,0:T(8,128)} %constant.9.clone.ral, ...), custom_call_target="tpu_custom_call" | custom-call | tf_op jit(solution)/shard_map/substep/pallas_call | solution.py:336
  108.4 0.9 copy.13
  109.3 0.7 copy.14

commit v4 on v3

--- a/solution.py
+++ b/solution.py
@@ -14,6 +14,7 @@
 ROWS, NZ, HALF = 48, 1536, 768
 LANES, SPLIT, MK, ST = 128, 512, 1024, 8
 PARTS = NZ // SPLIT
+GROUPS = ((0, 2), (2, 1))
 
 
 def bf16_parts(values):
@@ -97,16 +98,23 @@
         lax.fori_loop(0, NG - 1, step, 0)
         to_pen(pen_peer(NP - 1))
 
-    def arrived(target, count, phase):
-        ref = target.at[pl.ds(0, count - 1)]
+    def pen_block(ref, slot, group):
+        return ref.at[slot, pl.ds(*GROUPS[group])]
+
+    def grp_block(ref, slot, group):
+        first, size = GROUPS[group]
+        return ref.at[slot, :, pl.ds(first * LANES, size * LANES)]
+
+    def arrived(ref, phase):
         pltpu.make_async_copy(ref, ref, rsem.at[phase]).wait()
 
-    def sent(source, count, phase):
-        ref = source.at[pl.ds(0, count - 1)]
+    def sent(ref, phase):
         pltpu.make_async_copy(ref, ref, ssem.at[phase]).wait()
 
-    def mine(c, i):
-        return flow.at[lax.div(i, 4), :, pl.ds(pl.multiple_of((lax.rem(i, 4) + 4 * c) * LANES, LANES), LANES)]
+    def mine(i, group):
+        first, size = GROUPS[group]
+        start = pl.multiple_of((4 * first + size * lax.rem(i, 4)) * LANES, LANES)
+        return flow.at[lax.div(i, 4), :, pl.ds(start, size * LANES)]
 
     fetch = pltpu.make_async_copy(source, flow, fsem)
     fetch.start()
@@ -118,18 +126,18 @@
         for tile in range(16):
             cols = pl.ds((4 * c + tile % 4) * LANES, LANES)
             top, low = flow[tile // 4, :24, cols], flow[tile // 4, 24:, cols]
-            psend[c, 2 * tile] = jnp.where(lane, top, swap(low))
-            psend[c, 2 * tile + 1] = jnp.where(lane, swap(top), low)
+            psend[2 * tile, c] = jnp.where(lane, top, swap(low))
+            psend[2 * tile + 1, c] = jnp.where(lane, swap(top), low)
 
     pl.semaphore_wait(barrier, NP - 1 + NG - 1)
-    for c in range(PARTS):
+    for group, (first, size) in enumerate(GROUPS):
         exchange(
-            lambda peer: push("pen", peer, psend.at[c, peer], precv.at[c, me_p], c),
-            lambda peer: push("grp", peer, mine(c, peer), grecv.at[c, me_g], PARTS + c),
+            lambda peer: push("pen", peer, pen_block(psend, peer, group), pen_block(precv, me_p, group), group),
+            lambda peer: push("grp", peer, mine(peer, group), grp_block(grecv, me_g, group), 2 + group),
         )
-    for c in range(PARTS):
-        precv[c, me_p] = psend[c, me_p]
-        grecv[c, me_g] = mine(c, me_g)[...]
+    precv[me_p] = psend[me_p]
+    for group, (first, size) in enumerate(GROUPS):
+        grecv[me_g, :, pl.ds(first * LANES, size * LANES)] = mine(me_g, group)[...]
 
     def fill(b, carry):
         rows = pl.ds(pl.multiple_of(b * 16, 16), 16)
@@ -178,12 +186,13 @@
         fluid[:, pl.ds(zt * LANES, LANES)] = dot(open_cells, jnp.ones((ROWS, LANES), BF16))
 
     upper, scale = elimination()
-    for c in range(PARTS):
-        arrived(grecv.at[c], NG, PARTS + c)
+    for group, (first, size) in enumerate(GROUPS):
+        arrived(grp_block(grecv, pl.ds(0, NG - 1), group), 2 + group)
 
         def lines(t, carry):
-            rows = pl.ds(pl.multiple_of(t * 8, 8), 8)
-            f = [grecv[c, i, rows, :] for i in range(NG)]
+            rows = pl.ds(pl.multiple_of(lax.div(t, size) * 8, 8), 8)
+            cols = pl.ds(pl.multiple_of((first + lax.rem(t, size)) * LANES, LANES), LANES)
+            f = [grecv[i, rows, cols] for i in range(NG)]
             get = lambda i: f[i] if 0 <= i < NG else jnp.zeros_like(f[0])
             done = []
             for i in range(NG):
@@ -192,59 +201,65 @@
                     value = (value - done[-1] * (1.0 / 3.0)) * scale[i]
                 done.append(value)
             value = done[-1]
-            gmid[c, NG - 1, rows, :] = value
+            gmid[NG - 1, rows, cols] = value
             for i in reversed(range(NG - 1)):
                 value = done[i] - upper[i] * value
-                gmid[c, i, rows, :] = value
+                gmid[i, rows, cols] = value
             return carry
-        lax.fori_loop(0, ROWS // 8, lines, 0)
-        gback[c, me_g] = gmid[c, me_g]
-
-        arrived(precv.at[c], NP, c)
-
-        def halves(q, carry):
-            rows = pl.ds(pl.multiple_of(q * ROWS, 16), ROWS)
-            one, two = precv[c, q], precv[c, q + NP // 2]
-            for both, packed in ((fsum, one + two), (fdif, one - two)):
-                value = jnp.concatenate([packed, swap(packed)], axis=0)
-                high = value.astype(BF16).astype(F32)
-                both[rows, :] = jnp.where(wide < LANES // 2, high, swap(value - high)).astype(BF16)
-            return carry
-        lax.fori_loop(0, NP // 2, halves, 0)
-
-        def across(m, carry):
-            rows = pl.ds(pl.multiple_of(m * 256, 256), 256)
-            for out, high, low, both in ((ysum, tah, tal, fsum), (ydif, tbh, tbl, fdif)):
-                value = dot(high[rows, :], both[...])
-                out[rows, :] = value + swap(value) + dot(low[rows, :], both[...])
-            return carry
-        lax.fori_loop(0, 3, across, 0)
-
-        def pieces(q, carry):
-            rows = pl.ds(pl.multiple_of(q * ROWS, 8), ROWS)
-            total, other = ysum[rows, :], ydif[rows, :]
-            for slot, value in ((q, total + other), (q + NP // 2, total - other)):
-                pmid[c, slot] = jnp.where(lane, value[:24], swap(value[24:]))
-            return carry
-        lax.fori_loop(0, NP // 2, pieces, 0)
+        lax.fori_loop(0, ROWS // 8 * size, lines, 0)
+
+        arrived(pen_block(precv, pl.ds(0, NP - 1), group), group)
+        for c in range(first, first + size):
+            def halves(q, carry):
+                rows = pl.ds(pl.multiple_of(q * ROWS, 16), ROWS)
+                one, two = precv[q, c], precv[q + NP // 2, c]
+                for both, packed in ((fsum, one + two), (fdif, one - two)):
+                    value = jnp.concatenate([packed, swap(packed)], axis=0)
+                    high = value.astype(BF16).astype(F32)
+                    both[rows, :] = jnp.where(wide < LANES // 2, high, swap(value - high)).astype(BF16)
+                return carry
+            lax.fori_loop(0, NP // 2, halves, 0)
+
+            def across(m, carry):
+                rows = pl.ds(pl.multiple_of(m * 256, 256), 256)
+                for out, high, low, both in ((ysum, tah, tal, fsum), (ydif, tbh, tbl, fdif)):
+                    value = dot(high[rows, :], both[...])
+                    out[rows, :] = value + swap(value) + dot(low[rows, :], both[...])
+                return carry
+            lax.fori_loop(0, 3, across, 0)
+
+            def pieces(q, carry):
+                rows = pl.ds(pl.multiple_of(q * ROWS, 8), ROWS)
+                total, other = ysum[rows, :], ydif[rows, :]
+                for slot, value in ((q, total + other), (q + NP // 2, total - other)):
+                    pmid[slot, c] = jnp.where(lane, value[:24], swap(value[24:]))
+                return carry
+            lax.fori_loop(0, NP // 2, pieces, 0)
         exchange(
-            lambda peer: push("pen", peer, pmid.at[c, peer], pback.at[c, me_p], 2 * PARTS + c),
-            lambda peer: push("grp", peer, gmid.at[c, peer], gback.at[c, me_g], 3 * PARTS + c),
+            lambda peer: push("pen", peer, pen_block(pmid, peer, group), pen_block(pback, me_p, group), 4 + group),
+            lambda peer: push("grp", peer, grp_block(gmid, peer, group), grp_block(gback, me_g, group), 6 + group),
         )
-        pback[c, me_p] = pmid[c, me_p]
+        cols = pl.ds(first * LANES, size * LANES)
+        gback[me_g, :, cols] = gmid[me_g, :, cols]
+        for c in range(first, first + size):
+            pback[me_p, c] = pmid[me_p, c]
 
     count = 3 * lax.broadcasted_iota(jnp.int32, (ROWS, MK), 0)
     acc[...] = jnp.zeros_like(acc)
     corr[...] = jnp.zeros_like(corr)
     for c in range(PARTS):
-        arrived(gback.at[c], NG, 3 * PARTS + c)
-        arrived(pback.at[c], NP, 2 * PARTS + c)
+        for group, (first, size) in enumerate(GROUPS):
+            if c == first:
+                arrived(grp_block(gback, pl.ds(0, NG - 1), group), 6 + group)
+                arrived(pen_block(pback, pl.ds(0, NP - 1), group), 4 + group)
         for k in range(4):
             cols = pl.ds((4 * c + k) * LANES, LANES)
-            d0 = [gback[c, 4 * f + k] for f in range(4)]
+            first, size = next(g for g in GROUPS if g[0] <= c < sum(g))
+            at, lag = divmod(4 * (c - first) + k, size)
+            d0 = [gback[4 * f + at, :, pl.ds((first + lag) * LANES, LANES)] for f in range(4)]
             d1 = []
             for f in range(4):
-                one, two = pback[c, 8 * f + 2 * k], pback[c, 8 * f + 2 * k + 1]
+                one, two = pback[8 * f + 2 * k, c], pback[8 * f + 2 * k + 1, c]
                 d1.append(jnp.concatenate([jnp.where(lane, one, swap(two)), jnp.where(lane, swap(one), two)], axis=0))
             u0, u1 = flow[0, :, cols], flow[1, :, cols]
             for i in range(3):
@@ -272,7 +287,7 @@
 
             def spread_out(t, carry):
                 peer = grp_peer(t)
-                push("grp", peer, dsend.at[peer], drecv.at[me_g], 4 * PARTS)
+                push("grp", peer, dsend.at[peer], drecv.at[me_g], 8)
                 return carry
             lax.fori_loop(0, NG - 1, spread_out, 0)
             drecv[me_g] = dsend[me_g]
@@ -318,15 +333,15 @@
             part = corr[pl.ds((zt // 4 * 3 + i) * ROWS, ROWS), pl.ds(zt % 4 * LANES, LANES)]
             vel[i, :, cols] = fluid[:, cols] * (prov[i, :, cols] - part)
 
-    arrived(drecv, NG, 4 * PARTS)
+    arrived(drecv.at[pl.ds(0, NG - 1)], 8)
     pois[...] = drecv[:, :, :96]
 
-    for c in range(PARTS):
-        sent(psend.at[c], NP, c)
-        sent(grecv.at[c], NG, PARTS + c)
-        sent(pmid.at[c], NP, 2 * PARTS + c)
-        sent(gmid.at[c], NG, 3 * PARTS + c)
-    sent(dsend, NG, 4 * PARTS)
+    for group in range(len(GROUPS)):
+        sent(pen_block(psend, pl.ds(0, NP - 1), group), group)
+        sent(grp_block(grecv, pl.ds(0, NG - 1), group), 2 + group)
+        sent(pen_block(pmid, pl.ds(0, NP - 1), group), 4 + group)
+        sent(grp_block(gmid, pl.ds(0, NG - 1), group), 6 + group)
+    sent(dsend.at[pl.ds(0, NG - 1)], 8)
 
 
 def body(flow_fields, marker_cells, marker_weights, solid_blocks):
@@ -344,8 +359,8 @@
         out_specs=(vmem, vmem),
         scratch_shapes=[
             V((4, ROWS, NZ), F32),
-            *[V((PARTS, NP, ROWS // 2, LANES), F32)] * 4,
-            *[V((PARTS, NG, ROWS, LANES), F32)] * 3,
+            *[V((NP, PARTS, ROWS // 2, LANES), F32)] * 4,
+            *[V((NG, ROWS, PARTS * LANES), F32)] * 3,
             V((NG, ROWS, LANES), F32), V((NG, ROWS, LANES), F32),
             V((HALF, HALF), BF16), V((HALF, HALF), BF16), V((HALF, HALF), BF16), V((HALF, HALF), BF16),
             V((4 * ROWS, HALF), BF16), V((4 * ROWS, HALF), BF16), V((4 * ROWS, HALF), BF16), V((4 * ROWS, HALF), BF16),
@@ -353,7 +368,7 @@
             V((3, ROWS, NZ), F32), V((ROWS, NZ), F32), V((3, ROWS, NZ), F32),
             V((9 * ROWS, SPLIT), BF16), V((9 * ROWS, SPLIT), BF16),
             V((ST, SPLIT, MK), BF16), V((9 * ROWS, SPLIT), F32), V((3, 8, MK), F32), V((ROWS, NZ), F32),
-            pltpu.SemaphoreType.DMA((4 * PARTS + 1,)), pltpu.SemaphoreType.DMA((4 * PARTS + 1,)),
+            pltpu.SemaphoreType.DMA((9,)), pltpu.SemaphoreType.DMA((9,)),
             pltpu.SemaphoreType.DMA,
         ],
         compiler_params=pltpu.CompilerParams(

time: 110 us -> 113 us (1.027)
  Pallas kernels: 108 us -> 110 us
    pallas_call x1, Pallas kernels: 108 us -> 110 us  [body(): pl.pallas_call(kernel, name='substep', out_shape=(pltpu.VMEM((3, ROWS, NZ...]
where the time goes in v4:
time: 113 us
  Pallas kernels  110 us (97%)
  local copies, waits for them, and re-layouts  1.66 us (1%)
    pallas_call x1, Pallas kernels, body(): pl.pallas_call(kernel, name='substep', out_shape=(pltpu.VMEM((3, ROWS, NZ...  110 us

profile of v4, /device:TPU:1, one launch (start us, length us, event | category | flops | bytes accessed | tf_op | source)
XLA Modules:
  0.0 112.8 jit_solution(10847545025917163081)
XLA Ops:
  0.6 110.5 %substep.1 = (f32[3,48,1536]{2,1,0:T(8,128)S(1)}, f32[16,48,96]{2,1,0:T(8,128)S(1)}) custom-call(f32[4,48,1536]{2,1,0:T(8,128)} %bitcast.12, s32[8,1024]{1,0:T(8,128)} %bitcast.13, f32[8,1024]{1,0:T(8,128)} %bitcast.14, s32[12,1,48]{2,1,0:T(1,128)} %bitcast.15, f32[16,768]{1,0:T(8,128)} %constant.8.clone.rah, f32[16,768]{1,0:T(8,128)} %constant.9.clone.ral, ...), custom_call_target="tpu_custom_call" | custom-call | tf_op jit(solution)/shard_map/substep/pallas_call | solution.py:351
  111.1 0.9 copy.13
  112.0 0.7 copy.14

commit v5 on v3

--- a/solution.py
+++ b/solution.py
@@ -287,7 +287,7 @@
                 picked = jnp.where(mask, got[i * ROWS:(i + 1) * ROWS], 0.0)
                 acc[i] += jnp.sum(picked.reshape(6, 8, MK), axis=0) * weight
             return carry
-        lax.fori_loop(0, ST, sample, 0)
+        lax.fori_loop(0, ST, sample, 0, unroll=8)
 
     sampled = [jnp.sum(acc[i], axis=0, keepdims=True) for i in range(3)]
 
@@ -310,7 +310,7 @@
             total = value if total is None else total + value
         corr[...] += total
         return carry
-    lax.fori_loop(0, ST, spread, 0)
+    lax.fori_loop(0, ST, spread, 0, unroll=2)
 
     for zt in range(12):
         cols = pl.ds(zt * LANES, LANES)

time: 110 us -> 108 us (0.982)
  Pallas kernels: 108 us -> 106 us
    pallas_call x1, Pallas kernels: 108 us -> 106 us  [body(): pl.pallas_call(kernel, name='substep', out_shape=(pltpu.VMEM((3, ROWS, NZ...]
where the time goes in v5:
time: 108 us
  Pallas kernels  106 us (98%)
  local copies, waits for them, and re-layouts  1.66 us (2%)
    pallas_call x1, Pallas kernels, body(): pl.pallas_call(kernel, name='substep', out_shape=(pltpu.VMEM((3, ROWS, NZ...  106 us

profile of v5, /device:TPU:1, one launch (start us, length us, event | category | flops | bytes accessed | tf_op | source)
XLA Modules:
  0.0 108.1 jit_solution(2920432875392043077)
XLA Ops:
  0.6 105.8 %substep.1 = (f32[3,48,1536]{2,1,0:T(8,128)S(1)}, f32[16,48,96]{2,1,0:T(8,128)S(1)}) custom-call(f32[4,48,1536]{2,1,0:T(8,128)} %bitcast.12, s32[8,1024]{1,0:T(8,128)} %bitcast.13, f32[8,1024]{1,0:T(8,128)} %bitcast.14, s32[12,1,48]{2,1,0:T(1,128)} %bitcast.15, f32[16,768]{1,0:T(8,128)} %constant.8.clone.rah, f32[16,768]{1,0:T(8,128)} %constant.9.clone.ral, ...), custom_call_target="tpu_custom_call" | custom-call | tf_op jit(solution)/shard_map/substep/pallas_call | solution.py:336
  106.4 0.9 copy.13
  107.4 0.7 copy.14
